TPU v7x, 32 devices: a whole 2x2x4 slice. The times are simulated.
32 devices in a mesh: groups: 2 (over y), seq: 4 (over z), mp: 2 (over x), rep: 2 (over core).
Axes of the slice: x: 2, y: 2, z: 4, core: 2. Of those that a mesh axis runs over, the one named last changes fastest.
Arguments:
- encoder_rows: bfloat16 [8, 512, 4096], P('groups', ('seq', 'rep'), 'mp'), parts along dimension 0
- norm_gain: bfloat16 [4096], replicated, may hold values from 0.099609375 to 1.8984375
- key_weight: bfloat16 [4096, 2048], P(None, 'mp'), may hold values from -0.09375 to 0.09375
- value_weight: bfloat16 [4096, 2048], P(None, 'mp'), may hold values from -0.09375 to 0.09375
- queries: bfloat16 [64, 512, 2048], P(('groups', 'seq', 'rep'), None, 'mp'), parts along dimension 0
- wild_lengths: int32 [8], P('groups'), parts along dimension 0, may hold values from 128 to 512, as said below
- variant_counts: int32 [8], P('groups'), parts along dimension 0, may hold values from 4 to 12, as said below
Outputs:
- context: bfloat16 [64, 512, 2048], P(('groups', 'seq', 'rep'), None, 'mp'), parts along dimension 0
There are 2 independent parts, one for each index of `groups`. A program takes and returns all parts, laid end to end along the dimension named above; an argument that names none is the same for every part. Nothing has to cross between parts.
Inputs may be any that keep to these rules, and one draw needn't show every extreme that they name: `variant_counts`: the counts sum to 32; every wild type has at least 4 and at most 12 variants, and both ends are reached. Variants fill the slots in order of wild type, 4 slots to a device in the order of seq+rep, so one device's slots name at most two wild types; when 4 > 1 some device's slots name two. `wild_lengths`: some wild type has length 512.
All inputs are finite; a program needn't handle non-finite values.
Results may differ from a plain program's by a relative error of at most 0.0018.
The roundings to bfloat16 on the way count: a program that leaves them out, or rounds other values in their place, can miss the bound.
Values may be sent and summed in bfloat16 or wider, within the bound.
A program may use at most 128 MiB of HBM per device.

v0:
```python
import jax
import jax.numpy as jnp
from jax import lax
from jax.sharding import PartitionSpec as P

D = 4096
HD = 64
LEN = 512


def wild_of_slots(variant_counts, slot_total):
    running_end = jnp.cumsum(variant_counts)
    slot_number = jnp.arange(slot_total, dtype=jnp.int32)
    return jnp.sum((running_end[None, :] <= slot_number[:, None]).astype(jnp.int32), axis=1)


def projector(key_weight, value_weight, gain_wide, piece):
    width = piece.shape[2]
    flat_piece = piece.reshape(-1, width).astype(jnp.float32)
    gained = (flat_piece * gain_wide[None, :]).astype(jnp.bfloat16)
    key_total = jnp.dot(gained, key_weight, preferred_element_type=jnp.float32)
    value_total = jnp.dot(gained, value_weight, preferred_element_type=jnp.float32)
    return (key_total, value_total)


def local(encoder_rows, norm_gain, key_weight, value_weight, queries, wild_lengths, variant_counts):
    wild_total, part_length, part_width = encoder_rows.shape
    row_total = wild_total * part_length
    inner_local = key_weight.shape[1]
    head_local = inner_local // HD
    seq_size = lax.axis_size("seq")
    rep_size = lax.axis_size("rep")
    peer_total = seq_size * rep_size
    slot_local = queries.shape[0]
    slot_wild = wild_of_slots(variant_counts, peer_total * slot_local)
    by_device = slot_wild.reshape(peer_total, slot_local)
    own_index = lax.axis_index("seq") * rep_size + lax.axis_index("rep")
    own_wild = lax.dynamic_slice_in_dim(by_device, own_index, 1, 0)[0]
    gain_wide = norm_gain.astype(jnp.float32)
    local_flat = encoder_rows.reshape(row_total, part_width).astype(jnp.float32)
    square_sum = lax.psum(jnp.sum(local_flat * local_flat, axis=1), "mp")
    key_total, value_total = projector(
        key_weight, value_weight, gain_wide, lax.all_gather(encoder_rows, "mp", axis=2, tiled=True)
    )
    inverse_rms = lax.rsqrt(square_sum / D + 1e-06)[:, None]
    key_rows = (inverse_rms * key_total).astype(jnp.bfloat16)
    value_rows = (inverse_rms * value_total).astype(jnp.bfloat16)
    paired = jnp.concatenate([key_rows, value_rows], axis=1).reshape(
        wild_total, part_length, 2 * inner_local
    )
    wanted = jnp.stack([by_device[:, 0], by_device[:, slot_local - 1]])
    outgoing = paired[wanted]
    bundle = outgoing.shape[0]
    incoming = lax.all_to_all(outgoing, ("seq", "rep"), split_axis=1, concat_axis=1, tiled=True)
    incoming = incoming.reshape(bundle, LEN, 2 * inner_local)
    later = jnp.minimum((own_wild != own_wild[0]).astype(jnp.int32), bundle - 1)
    slot_pairs = incoming[later]
    wild_number = jnp.arange(wild_lengths.shape[0], dtype=jnp.int32)
    own_lengths = jnp.sum(
        jnp.where(own_wild[:, None] == wild_number[None, :], wild_lengths[None, :], 0), axis=1
    )
    positions = jnp.arange(LEN, dtype=jnp.int32)

    def attend_slot(packed):
        query_rows, pair_rows, seq_length = packed
        query_heads = query_rows.reshape(LEN, head_local, HD)
        key_heads = pair_rows[:, :inner_local].reshape(LEN, head_local, HD)
        value_heads = pair_rows[:, inner_local:].reshape(LEN, head_local, HD)
        scores = jnp.einsum(
            "qhd,khd->hqk", query_heads, key_heads, preferred_element_type=jnp.float32
        )
        validity = positions < seq_length
        scores = jnp.where(validity[None, None, :], scores, jnp.float32(-1e30))
        maximum = jnp.max(scores, axis=2, keepdims=True)
        weights = jnp.exp(scores - maximum)
        softmax_weights = (weights / jnp.sum(weights, axis=2, keepdims=True)).astype(jnp.bfloat16)
        outcome = jnp.einsum(
            "hqk,khd->qhd", softmax_weights, value_heads, preferred_element_type=jnp.float32
        )
        outcome = jnp.where(validity[:, None, None], outcome, jnp.float32(0.0))
        return outcome.reshape(LEN, inner_local).astype(jnp.bfloat16)

    return lax.map(attend_slot, (queries, slot_pairs, own_lengths))


def solution(mesh):
    placed = (
        P("groups", ("seq", "rep"), "mp"),
        P(),
        P(None, "mp"),
        P(None, "mp"),
        P(("groups", "seq", "rep"), None, "mp"),
        P("groups"),
        P("groups"),
    )
    return jax.shard_map(
        local,
        mesh=mesh,
        in_specs=placed,
        out_specs=P(("groups", "seq", "rep"), None, "mp"),
        check_vma=False,
    )
```

profile of v0, /device:TPU:29, one launch (start us, length us, event | category | flops | bytes accessed | tf_op | source)
XLA Modules:
  0.0 304.8 jit_solution(6685066232856983752)
XLA Ops:
  9.3 1.5 multiply_reduce_fusion
  10.9 3.8 %psum.7 = f32[256]{0:T(256)S(1)} all-reduce(f32[256]{0:T(256)S(1)} %reduce_sum.41), channel_id=1, replica_groups=mesh['groups'=2,'seq'=4,'mp'=2,'rep'=2] {'mp'}, use_global_device_ids=true, to_apply=%region_1.2 | all-reduce | flops 256 | bytes 2048 | tf_op jit(solution)/shard_map/psum | solution.py:41
  14.6 28.3 %all-gather.2.cloned.1.call-done = bf16[4,64,4096]{2,1,0:T(8,128)(2,1)} async-done(((bf16[4,64,2048]{2,1,0:T(8,128)(2,1)}), bf16[4,64,4096]{2,1,0:T(8,128)(2,1)}) %all-gather.2.cloned.1.call-update) | async-done | bytes 2097168 | tf_op jit(solution)/shard_map/all_gather | solution.py:43
  43.0 2.3 fusion.12
  45.3 5.9 %fusion.13 = bf16[256,1024]{1,0:T(8,128)(2,1)S(1)} fusion(bf16[256,4096]{1,0:T(8,128)(2,1)S(1)} %fusion.12, bf16[4096,1024]{1,0:T(8,128)(2,1)} %param.11, f32[256]{0:T(256)S(1)} %add_rsqrt_fusion), kind=kOutput, calls=%fused_computation.25 | convolution fusion | flops 2148007936 | bytes 11011072 | tf_op jit(solution)/shard_map/dot_general | solution.py:21
  51.3 2.4 fusion.14
  53.7 2.8 gather_fusion
  56.6 4.7 %copy.27 = bf16[2,8,64,2048]{3,2,0,1:T(8,128)(2,1)} copy(bf16[2,8,64,2048]{3,2,1,0:T(8,128)(2,1)} %bitcast.64) | data formatting | bytes 8388608 | tf_op jit(solution)/shard_map/gather | solution.py:52
  61.3 5.5 %all-to-all-start = ((bf16[2,8,64,2048]{3,2,0,1:T(8,128)(2,1)}), bf16[2,8,64,2048]{3,2,0,1:T(8,128)(2,1)}, u32[]{:S(2)}, u32[]{:S(2)}) async-start(bf16[2,8,64,2048]{3,2,0,1:T(8,128)(2,1)} %copy.27), calls=%async_computation | async-start | bytes 8388608 | tf_op jit(solution)/shard_map/all_to_all | solution.py:54
  67.1 91.2 %all-to-all-done = bf16[2,8,64,2048]{3,2,0,1:T(8,128)(2,1)} async-done(((bf16[2,8,64,2048]{3,2,0,1:T(8,128)(2,1)}), bf16[2,8,64,2048]{3,2,0,1:T(8,128)(2,1)}, u32[]{:S(2)}, u32[]{:S(2)}) %all-to-all-start) | async-done | bytes 4194336 | tf_op jit(solution)/shard_map/all_to_all | solution.py:54
  158.3 2.5 copy.28
  160.8 1.8 fusion.21
  162.6 4.3 %gather_fusion.1 = bf16[4,512,1024]{2,1,0:T(8,128)(2,1)} fusion(bf16[2,512,1024]{2,1,0:T(8,128)(2,1)} %get-tuple-element.91, s32[1024]{0:T(1024)S(1)} %pad_clamp_fusion), kind=kCustom, calls=%fused_computation.1 | custom fusion | bytes 8388624 | tf_op jit(solution)/shard_map/gather | solution.py:57
  166.9 2.8 gather_fusion.2
  169.7 8.2 %pad_maximum_fusion = bf16[4,512,2048]{2,1,0:T(8,128)(2,1)} fusion(bf16[4,512,1024]{2,1,0:T(8,128)(2,1)} %gather_fusion.2, bf16[4,512,1024]{2,1,0:T(8,128)(2,1)} %gather_fusion.1), kind=kLoop, calls=%fused_computation.19 | loop fusion | flops 16777216 | bytes 16777216
  177.9 120.1 %while.11 = (s32[]{:T(128)}, bf16[4,512,1024]{2,1,0:T(8,128)(2,1)}, s32[4]{0:T(128)S(1)}, bf16[4,512,2048]{2,1,0:T(8,128)(2,1)}, bf16[4,512,1024]{2,1,0:T(8,128)(2,1)}, /*index=5*/s32[]{:T(128)}) while((s32[]{:T(128)}, bf16[4,512,1024]{2,1,0:T(8,128)(2,1)}, s32[4]{0:T(128)S(1)}, bf16[4,512,2048]{2,1,0:T(8,128)(2,1)}, ...), condition=%wide.region_8.9_spmd.clone, body=%wide.region_5.8_spmd.clone.sunk | while | flops 1095762944 | bytes 58787932 | solution.py:83
  177.9 3.2 %constant_dynamic-slice_fusion.5 = bf16[1,512,2048]{2,1,0:T(8,128)(2,1)} fusion(bf16[4,512,2048]{2,1,0:T(8,128)(2,1)} %get-tuple-element.147, s32[]{:T(128)} %get-tuple-element.138), kind=kLoop, calls=%fused_computation.17.clone.1 | loop fusion | bytes 4194308 | tf_op jit(solution)/shard_map/while/body/jit(dynamic_index_in_dim)/dynamic_slice | solution.py:83
  181.1 2.9 copy.40
  188.3 10.6 %fusion.41 = (f32[16,512]{1,0:T(8,128)S(1)}, f32[16,512,512]{1,2,0:T(8,128)}) fusion(pred[512]{0:T(512)(128)(4,1)S(1)} %iota_compare_fusion.4, bf16[512,16,64]{0,2,1:T(8,128)(2,1)S(1)} %bitcast.58, bf16[512,16,64]{0,2,1:T(8,128)(2,1)} %bitcast.62), kind=kOutput, calls=%fused_computation.46.clone.1 | convolution fusion | flops 549454336 | bytes 18907648 | tf_op jit(solution)/shard_map/while/body/eval_jaxpr/sub | solution.py:75
  198.9 7.4 %select_convert_fusion.2 = bf16[16,64,512]{2,1,0:T(8,128)(2,1)S(1)} fusion(bf16[512,16,64]{0,2,1:T(8,128)(2,1)S(1)} %bitcast.61, f32[16,512,512]{1,2,0:T(8,128)} %get-tuple-element.130, f32[16,512]{1,0:T(8,128)S(1)} %get-tuple-element.131, pred[512]{0:T(512)(128)(4,1)S(1)} %iota_compare_fusion.4), kind=kOutput, calls=%fused_computation.12.clone.1 | convolution fusion | flops 546308096 | bytes 18907648 | tf_op jit(solution)/shard_map/while/body/eval_jaxpr/hqk,khd->qhd/dot_general | solution.py:77
  207.9 3.2 %constant_dynamic-slice_fusion.5 = bf16[1,512,2048]{2,1,0:T(8,128)(2,1)} fusion(bf16[4,512,2048]{2,1,0:T(8,128)(2,1)} %get-tuple-element.147, s32[]{:T(128)} %get-tuple-element.138), kind=kLoop, calls=%fused_computation.17.clone.1 | loop fusion | bytes 4194308 | tf_op jit(solution)/shard_map/while/body/jit(dynamic_index_in_dim)/dynamic_slice | solution.py:83
  211.1 2.9 copy.40
  218.4 10.6 %fusion.41 = (f32[16,512]{1,0:T(8,128)S(1)}, f32[16,512,512]{1,2,0:T(8,128)}) fusion(pred[512]{0:T(512)(128)(4,1)S(1)} %iota_compare_fusion.4, bf16[512,16,64]{0,2,1:T(8,128)(2,1)S(1)} %bitcast.58, bf16[512,16,64]{0,2,1:T(8,128)(2,1)} %bitcast.62), kind=kOutput, calls=%fused_computation.46.clone.1 | convolution fusion | flops 549454336 | bytes 18907648 | tf_op jit(solution)/shard_map/while/body/eval_jaxpr/sub | solution.py:75
  229.0 7.4 %select_convert_fusion.2 = bf16[16,64,512]{2,1,0:T(8,128)(2,1)S(1)} fusion(bf16[512,16,64]{0,2,1:T(8,128)(2,1)S(1)} %bitcast.61, f32[16,512,512]{1,2,0:T(8,128)} %get-tuple-element.130, f32[16,512]{1,0:T(8,128)S(1)} %get-tuple-element.131, pred[512]{0:T(512)(128)(4,1)S(1)} %iota_compare_fusion.4), kind=kOutput, calls=%fused_computation.12.clone.1 | convolution fusion | flops 546308096 | bytes 18907648 | tf_op jit(solution)/shard_map/while/body/eval_jaxpr/hqk,khd->qhd/dot_general | solution.py:77
  237.9 3.2 %constant_dynamic-slice_fusion.5 = bf16[1,512,2048]{2,1,0:T(8,128)(2,1)} fusion(bf16[4,512,2048]{2,1,0:T(8,128)(2,1)} %get-tuple-element.147, s32[]{:T(128)} %get-tuple-element.138), kind=kLoop, calls=%fused_computation.17.clone.1 | loop fusion | bytes 4194308 | tf_op jit(solution)/shard_map/while/body/jit(dynamic_index_in_dim)/dynamic_slice | solution.py:83
  241.1 2.9 copy.40
  248.4 10.6 %fusion.41 = (f32[16,512]{1,0:T(8,128)S(1)}, f32[16,512,512]{1,2,0:T(8,128)}) fusion(pred[512]{0:T(512)(128)(4,1)S(1)} %iota_compare_fusion.4, bf16[512,16,64]{0,2,1:T(8,128)(2,1)S(1)} %bitcast.58, bf16[512,16,64]{0,2,1:T(8,128)(2,1)} %bitcast.62), kind=kOutput, calls=%fused_computation.46.clone.1 | convolution fusion | flops 549454336 | bytes 18907648 | tf_op jit(solution)/shard_map/while/body/eval_jaxpr/sub | solution.py:75
  259.0 7.4 %select_convert_fusion.2 = bf16[16,64,512]{2,1,0:T(8,128)(2,1)S(1)} fusion(bf16[512,16,64]{0,2,1:T(8,128)(2,1)S(1)} %bitcast.61, f32[16,512,512]{1,2,0:T(8,128)} %get-tuple-element.130, f32[16,512]{1,0:T(8,128)S(1)} %get-tuple-element.131, pred[512]{0:T(512)(128)(4,1)S(1)} %iota_compare_fusion.4), kind=kOutput, calls=%fused_computation.12.clone.1 | convolution fusion | flops 546308096 | bytes 18907648 | tf_op jit(solution)/shard_map/while/body/eval_jaxpr/hqk,khd->qhd/dot_general | solution.py:77
  267.9 3.2 %constant_dynamic-slice_fusion.5 = bf16[1,512,2048]{2,1,0:T(8,128)(2,1)} fusion(bf16[4,512,2048]{2,1,0:T(8,128)(2,1)} %get-tuple-element.147, s32[]{:T(128)} %get-tuple-element.138), kind=kLoop, calls=%fused_computation.17.clone.1 | loop fusion | bytes 4194308 | tf_op jit(solution)/shard_map/while/body/jit(dynamic_index_in_dim)/dynamic_slice | solution.py:83
  271.1 2.9 copy.40
  278.4 10.6 %fusion.41 = (f32[16,512]{1,0:T(8,128)S(1)}, f32[16,512,512]{1,2,0:T(8,128)}) fusion(pred[512]{0:T(512)(128)(4,1)S(1)} %iota_compare_fusion.4, bf16[512,16,64]{0,2,1:T(8,128)(2,1)S(1)} %bitcast.58, bf16[512,16,64]{0,2,1:T(8,128)(2,1)} %bitcast.62), kind=kOutput, calls=%fused_computation.46.clone.1 | convolution fusion | flops 549454336 | bytes 18907648 | tf_op jit(solution)/shard_map/while/body/eval_jaxpr/sub | solution.py:75
  289.0 7.4 %select_convert_fusion.2 = bf16[16,64,512]{2,1,0:T(8,128)(2,1)S(1)} fusion(bf16[512,16,64]{0,2,1:T(8,128)(2,1)S(1)} %bitcast.61, f32[16,512,512]{1,2,0:T(8,128)} %get-tuple-element.130, f32[16,512]{1,0:T(8,128)S(1)} %get-tuple-element.131, pred[512]{0:T(512)(128)(4,1)S(1)} %iota_compare_fusion.4), kind=kOutput, calls=%fused_computation.12.clone.1 | convolution fusion | flops 546308096 | bytes 18907648 | tf_op jit(solution)/shard_map/while/body/eval_jaxpr/hqk,khd->qhd/dot_general | solution.py:77
  (54 shorter events, 27.1 us)
Async XLA Ops:
  6.5 36.4 %all-gather.2.cloned.1.call-start = ((), (), s32[]{:S(2)}) async-start(), calls=%async_computation.1 | async-start | bytes 3145728 | tf_op jit(solution)/shard_map/all_gather | solution.py:43
  43.0 8.3 %slice-start = ((s8[8388608]{0:T(1024)(128)(4,1)}), s8[4194304]{0:T(1024)(128)(4,1)S(1)}, s32[]{:S(2)}) async-start(s8[8388608]{0:T(1024)(128)(4,1)} %bitcast.68), calls=%async_computation.2 | async-start | bytes 8388608
  45.3 6.0 %slice-start.1 = ((s8[8388608]{0:T(1024)(128)(4,1)}), s8[4194304]{0:T(1024)(128)(4,1)S(1)}, s32[]{:S(2)}) async-start(s8[8388608]{0:T(1024)(128)(4,1)} %bitcast.68), calls=%async_computation.3 | async-start | bytes 8388608
  61.3 5.6 %copy-start = (s32[4]{0:T(128)S(1)}, s32[4]{0:T(128)}, u32[]{:S(2)}) copy-start(s32[4]{0:T(128)} %param.14) | copy-start | bytes 52
  61.3 97.0 %all-to-all-start = ((bf16[2,8,64,2048]{3,2,0,1:T(8,128)(2,1)}), bf16[2,8,64,2048]{3,2,0,1:T(8,128)(2,1)}, u32[]{:S(2)}, u32[]{:S(2)}) async-start(bf16[2,8,64,2048]{3,2,0,1:T(8,128)(2,1)} %copy.27), calls=%async_computation | async-start | bytes 8388608 | tf_op jit(solution)/shard_map/all_to_all | solution.py:54
Sparse Core Ops, SparseCore 0:
  8.9 34.0 all-gather.1
where the time goes:
time: 310 us; the launch traced here: 305 us
  waiting for transfers between devices  120 us (39%)
  matrix products  80.1 us (26%)
  local copies, waits for them, and re-layouts  64.8 us (21%)
  other arithmetic  16.7 us (5%)
  between operations  13.5 us (4%)
  starting transfers between devices  5.55 us (2%)
  blocking collectives  3.77 us (1%)
    all_to_all x1, waiting for transfers between devices, local(): lax.all_to_all(outgoing, ('seq', 'rep'), split_axis=1, concat_axis=1, til...  91.2 us
    sub x4, matrix products, attend_slot(): weights = jnp.exp(scores - maximum)  42.4 us
    dynamic_slice x20, local copies, waits for them, and re-layouts, local(): return lax.map(attend_slot, (queries, slot_pairs, own_lengths))  34.2 us
    dot_general x4, matrix products, attend_slot(): jnp.einsum('hqk,khd->qhd', softmax_weights, value_heads, preferred_elemen...  29.4 us
    all_gather x1, waiting for transfers between devices, local(): lax.all_gather(encoder_rows, 'mp', axis=2, tiled=True)  28.3 us
    gather x3, local copies, waits for them, and re-layouts, local(): slot_pairs = incoming[later]  8.88 us
    unnamed x2, other arithmetic  8.15 us
    gather x2, local copies, waits for them, and re-layouts, local(): outgoing = paired[wanted]  7.57 us
  transfers between devices with their start and end apart: 2, of which 2 were waited for; matrix products, arithmetic and copies ran while one was open for 1% of the time, Pallas kernels for 0%

commit v1 on v0

v1 whole, which is shorter than its diff:
```python
import functools

import jax
import jax.numpy as jnp
from jax import lax
from jax.experimental import pallas as pl
from jax.experimental.pallas import tpu as pltpu
from jax.sharding import PartitionSpec as P

D = 4096
HD = 64
LEN = 512
PAIR = 2 * HD
Q_CHUNK = 256
HEAD_CHUNKS = 2


def wild_of_slots(variant_counts, slot_total):
    running_end = jnp.cumsum(variant_counts)
    slot_number = jnp.arange(slot_total, dtype=jnp.int32)
    return jnp.sum((running_end[None, :] <= slot_number[:, None]).astype(jnp.int32), axis=1)


def attend_kernel(wild_ref, length_ref, q_ref, k_ref, v_ref, *rest):
    o_ref = rest[-1]
    length = length_ref[pl.program_id(1)]
    keys = k_ref[...].reshape(LEN, PAIR)
    values = v_ref[...].reshape(LEN, PAIR)
    lane = lax.broadcasted_iota(jnp.int32, (Q_CHUNK, PAIR), 1)
    valid = lax.broadcasted_iota(jnp.int32, (Q_CHUNK, LEN), 1) < length
    for start in range(0, LEN, Q_CHUNK):
        query = q_ref[0, pl.ds(start, Q_CHUNK), :]
        outs = []
        for head in range(2):
            own_lanes = lane < HD if head == 0 else lane >= HD
            masked_query = jnp.where(own_lanes, query, jnp.zeros_like(query))
            scores = lax.dot_general(
                masked_query, keys, (((1,), (1,)), ((), ())), preferred_element_type=jnp.float32
            )
            scores = jnp.where(valid, scores, jnp.float32(-1e30))
            maximum = jnp.max(scores, axis=1, keepdims=True)
            weights = jnp.exp(scores - maximum)
            inverse = 1.0 / jnp.sum(weights, axis=1, keepdims=True)
            probs = (weights * inverse).astype(jnp.bfloat16)
            outs.append(jnp.dot(probs, values, preferred_element_type=jnp.float32))
        out = jnp.where(lane < HD, outs[0], outs[1])
        row = start + lax.broadcasted_iota(jnp.int32, (Q_CHUNK, PAIR), 0)
        o_ref[0, pl.ds(start, Q_CHUNK), :] = jnp.where(row < length, out, 0.0).astype(o_ref.dtype)


def attend(own_wild, own_lengths, queries, gathered, previous, chunk):
    slots, _, inner = queries.shape
    peers, _, part, double = gathered.shape
    pairs = double // 2 // PAIR
    base = chunk * pairs
    kv_block = (peers, 1, part, PAIR)
    in_specs = [
        pl.BlockSpec((1, LEN, PAIR), lambda h, s, w, n: (s, 0, base + h)),
        pl.BlockSpec(kv_block, lambda h, s, w, n: (0, w[s], 0, h)),
        pl.BlockSpec(kv_block, lambda h, s, w, n: (0, w[s], 0, pairs + h)),
    ]
    operands = [own_wild, own_lengths, queries, gathered, gathered]
    aliases = {}
    if previous is not None:
        in_specs.append(pl.BlockSpec(memory_space=pl.ANY))
        operands.append(previous)
        aliases = {5: 0}
    elements = slots * pairs * 2 * LEN * LEN
    return pl.pallas_call(
        attend_kernel,
        out_shape=jax.ShapeDtypeStruct(queries.shape, jnp.bfloat16),
        grid_spec=pltpu.PrefetchScalarGridSpec(
            num_scalar_prefetch=2,
            grid=(pairs, slots),
            in_specs=in_specs,
            out_specs=pl.BlockSpec((1, LEN, PAIR), lambda h, s, w, n: (s, 0, base + h)),
        ),
        input_output_aliases=aliases,
        compiler_params=pltpu.CompilerParams(vmem_limit_bytes=32 << 20),
        cost_estimate=pl.CostEstimate(
            flops=elements * 2 * PAIR * 2, transcendentals=elements, bytes_accessed=slots * pairs * LEN * PAIR * 8
        ),
    )(*operands)


def local(encoder_rows, norm_gain, key_weight, value_weight, queries, wild_lengths, variant_counts):
    wild_total, part_length, part_width = encoder_rows.shape
    row_total = wild_total * part_length
    inner_local = key_weight.shape[1]
    seq_size = lax.axis_size("seq")
    rep_size = lax.axis_size("rep")
    peer_total = seq_size * rep_size
    slot_local = queries.shape[0]
    slot_wild = wild_of_slots(variant_counts, peer_total * slot_local)
    own_index = lax.axis_index("seq") * rep_size + lax.axis_index("rep")
    own_wild = lax.dynamic_slice_in_dim(slot_wild, own_index * slot_local, slot_local, 0)
    wild_number = jnp.arange(wild_total, dtype=jnp.int32)
    own_lengths = jnp.sum(
        jnp.where(own_wild[:, None] == wild_number[None, :], wild_lengths[None, :], 0), axis=1
    )
    own_wild = jnp.minimum(own_wild, wild_total - 1)
    rows = lax.all_gather(encoder_rows, "mp", axis=2, tiled=True).reshape(row_total, -1).astype(jnp.float32)
    gained = (rows * norm_gain.astype(jnp.float32)[None, :]).astype(jnp.bfloat16)
    inverse_rms = lax.rsqrt(jnp.sum(rows * rows, axis=1) / D + 1e-06)[:, None]
    width = inner_local // HEAD_CHUNKS
    shared = []
    for chunk in range(HEAD_CHUNKS):
        columns = slice(chunk * width, (chunk + 1) * width)
        parts = []
        for weight in (key_weight, value_weight):
            total = jnp.dot(gained, weight[:, columns], preferred_element_type=jnp.float32)
            parts.append((inverse_rms * total).astype(jnp.bfloat16))
        paired = jnp.concatenate(parts, axis=1).reshape(wild_total, part_length, 2 * width)
        shared.append(lax.all_gather(paired, ("seq", "rep"), axis=0))
    context = None
    for chunk in range(HEAD_CHUNKS):
        context = attend(own_wild, own_lengths, queries, shared[chunk], context, chunk)
    return context


def solution(mesh):
    placed = (
        P("groups", ("seq", "rep"), "mp"),
        P(),
        P(None, "mp"),
        P(None, "mp"),
        P(("groups", "seq", "rep"), None, "mp"),
        P("groups"),
        P("groups"),
    )
    return jax.shard_map(
        local,
        mesh=mesh,
        in_specs=placed,
        out_specs=P(("groups", "seq", "rep"), None, "mp"),
        check_vma=False,
    )
```

time: 310 us -> 195 us (0.63)
  the two profiles are of different devices: /device:TPU:29 before, /device:TPU:1 now
where the time goes in v1:
time: 195 us
  waiting for transfers between devices  86.4 us (44%)
  Pallas kernels  65.4 us (34%)
  matrix products  14 us (7%)
  between operations  13.2 us (7%)
  local copies, waits for them, and re-layouts  8.85 us (5%)
  other arithmetic  7.16 us (4%)
    pallas_call x2, Pallas kernels, attend(): pl.pallas_call(attend_kernel, out_shape=jax.ShapeDtypeStruct(queries.shap...  65.4 us
    all_gather x2, waiting for transfers between devices, local(): shared.append(lax.all_gather(paired, ('seq', 'rep'), axis=0))  49.5 us
    all_gather x1, waiting for transfers between devices, local(): lax.all_gather(encoder_rows, 'mp', axis=2, tiled=True)  36.1 us
    dot_general x4, matrix products, local(): jnp.dot(gained, weight[:, columns], preferred_element_type=jnp.float32)  14 us
    unnamed x12, local copies, waits for them, and re-layouts  8.76 us
  transfers between devices with their start and end apart: 3, of which 3 were waited for; matrix products, arithmetic and copies ran while one was open for 5% of the time, Pallas kernels for 17%

profile of v1, /device:TPU:1, one launch (start us, length us, event | category | flops | bytes accessed | tf_op | source)
XLA Modules:
  0.0 195.0 jit_solution(17293583525154429726)
XLA Ops:
  6.5 0.0 all-gather.4.cloned.1.call-start
  6.5 0.7 all-gather.4.cloned.1.call-update
  7.3 0.0 all-gather.8.cloned.1.call-start
  7.3 0.7 convert_element_type.34
  8.0 36.1 %all-gather.4.cloned.1.call-done = bf16[4,64,4096]{2,1,0:T(8,128)(2,1)} async-done(((bf16[4,64,2048]{2,1,0:T(8,128)(2,1)}), bf16[4,64,4096]{2,1,0:T(8,128)(2,1)}) %all-gather.4.cloned.1.call-update) | async-done | bytes 2097168 | tf_op jit(solution)/shard_map/all_gather | solution.py:102
  44.1 2.1 %multiply_reduce_fusion = f32[4,64]{1,0:T(4,128)S(1)} fusion(bf16[4,64,4096]{2,1,0:T(8,128)(2,1)} %all-gather.4.cloned.1.call-done), kind=kLoop, calls=%fused_computation.10 | loop fusion | flops 3145472 | bytes 2098176 | tf_op jit(solution)/shard_map/reduce_sum | solution.py:104
  46.2 0.1 rsqrt.11
  46.3 2.1 %fusion = bf16[256,4096]{1,0:T(8,128)(2,1)S(1)} fusion(f32[4096]{0:T(1024)S(1)} %convert_element_type.34, bf16[4,64,4096]{2,1,0:T(8,128)(2,1)} %all-gather.4.cloned.1.call-done), kind=kLoop, calls=%fused_computation.1 | loop fusion | flops 3145728 | bytes 4210688 | tf_op jit(solution)/shard_map/convert_element_type | solution.py:103
  48.4 3.5 %fusion.21 = bf16[256,512]{1,0:T(8,128)(2,1)S(1)} fusion(bf16[256,4096]{1,0:T(8,128)(2,1)S(1)} %fusion, bf16[4096,1024]{1,0:T(8,128)(2,1)} %param.10, f32[256]{0:T(256)S(1)} %rsqrt.11), kind=kOutput, calls=%fused_computation.15 | convolution fusion | flops 1074003968 | bytes 6554624 | tf_op jit(solution)/shard_map/dot_general | solution.py:111
  51.9 3.5 %fusion.24 = bf16[256,512]{1,0:T(8,128)(2,1)S(1)} fusion(bf16[256,4096]{1,0:T(8,128)(2,1)S(1)} %fusion, bf16[4096,1024]{1,0:T(8,128)(2,1)} %param.9, f32[256]{0:T(256)S(1)} %rsqrt.11), kind=kOutput, calls=%fused_computation.16 | convolution fusion | flops 1074003968 | bytes 6554624 | tf_op jit(solution)/shard_map/dot_general | solution.py:111
  55.4 0.9 pad_maximum_fusion.1
  56.2 0.0 all-gather.8.cloned.1.call-update
  56.3 0.0 all-gather.6.cloned.1.call-start
  56.3 3.5 %fusion.27 = bf16[256,512]{1,0:T(8,128)(2,1)S(1)} fusion(bf16[256,4096]{1,0:T(8,128)(2,1)S(1)} %fusion, bf16[4096,1024]{1,0:T(8,128)(2,1)} %param.10, f32[256]{0:T(256)S(1)} %rsqrt.11), kind=kOutput, calls=%fused_computation.17 | convolution fusion | flops 1074003968 | bytes 6554624 | tf_op jit(solution)/shard_map/dot_general | solution.py:111
  59.8 0.0 copy-start.4
  59.8 0.0 copy-start.5
  59.8 3.5 %fusion.30 = bf16[256,512]{1,0:T(8,128)(2,1)S(1)} fusion(bf16[256,4096]{1,0:T(8,128)(2,1)S(1)} %fusion, bf16[4096,1024]{1,0:T(8,128)(2,1)} %param.9, f32[256]{0:T(256)S(1)} %rsqrt.11), kind=kOutput, calls=%fused_computation.18 | convolution fusion | flops 1074003968 | bytes 6554624 | tf_op jit(solution)/shard_map/dot_general | solution.py:111
  63.3 0.9 pad_maximum_fusion
  64.2 0.0 all-gather.6.cloned.1.call-update
  64.3 0.2 reduce-window.8
  64.5 0.1 convert_reduce_fusion
  64.6 0.1 broadcast_minimum_fusion
  64.6 0.0 copy-done.5
  64.6 0.2 select_reduce_fusion.length_ref
  64.8 38.9 %all-gather.8.cloned.1.call-done.k_ref.v_ref = bf16[8,4,64,1024]{3,2,1,0:T(8,128)(2,1)} async-done(((bf16[1,4,64,1024]{3,2,1,0:T(8,128)(2,1)}), bf16[8,4,64,1024]{3,2,1,0:T(8,128)(2,1)}) %all-gather.8.cloned.1.call-update) | async-done | bytes 4194320 | tf_op jit(solution)/shard_map/all_gather | solution.py:114
  103.8 2.2 %copy-done = bf16[4,512,1024]{2,1,0:T(8,128)(2,1)S(1)} copy-done((bf16[4,512,1024]{2,1,0:T(8,128)(2,1)S(1)}, bf16[4,512,1024]{2,1,0:T(8,128)(2,1)}, u32[]{:S(2)}) %copy-start) | copy-done | bytes 4194328
  105.9 2.2 %copy-done.2 = bf16[8,4,64,1024]{3,2,1,0:T(8,128)(2,1)S(1)} copy-done((bf16[8,4,64,1024]{3,2,1,0:T(8,128)(2,1)S(1)}, bf16[8,4,64,1024]{3,2,1,0:T(8,128)(2,1)}, u32[]{:S(2)}) %copy-start.2) | copy-done | bytes 4194328
  108.1 32.7 %shard_map.73.rest_0_ = bf16[4,512,1024]{2,1,0:T(8,128)(2,1)} custom-call(s32[4]{0:T(128)S(1)} %get-tuple-element.5.wild_ref, s32[4]{0:T(128)S(1)} %select_reduce_fusion.length_ref, bf16[4,512,1024]{2,1,0:T(8,128)(2,1)S(1)} %copy-done, bf16[8,4,64,1024]{3,2,1,0:T(8,128)(2,1)S(1)} %copy-done.2, bf16[8,4,64,1024]{3,2,1,0:T(8,128)(2,1)S(1)} %copy-done.2), custom_call_target="tpu_custom_call" | custom-call | flops 4294967296 | bytes 8388608 | tf_op jit(solution)/shard_map/pallas_call | solution.py:69
  140.8 10.5 %all-gather.6.cloned.1.call-done.k_ref.v_ref = bf16[8,4,64,1024]{3,2,1,0:T(8,128)(2,1)} async-done(((bf16[1,4,64,1024]{3,2,1,0:T(8,128)(2,1)}), bf16[8,4,64,1024]{3,2,1,0:T(8,128)(2,1)}) %all-gather.6.cloned.1.call-update) | async-done | bytes 4194320 | tf_op jit(solution)/shard_map/all_gather | solution.py:114
  151.4 2.2 %copy-done.1 = bf16[4,512,1024]{2,1,0:T(8,128)(2,1)S(1)} copy-done((bf16[4,512,1024]{2,1,0:T(8,128)(2,1)S(1)}, bf16[4,512,1024]{2,1,0:T(8,128)(2,1)}, u32[]{:S(2)}) %copy-start.1) | copy-done | bytes 4194328
  153.6 2.2 %copy-done.3 = bf16[8,4,64,1024]{3,2,1,0:T(8,128)(2,1)S(1)} copy-done((bf16[8,4,64,1024]{3,2,1,0:T(8,128)(2,1)S(1)}, bf16[8,4,64,1024]{3,2,1,0:T(8,128)(2,1)}, u32[]{:S(2)}) %copy-start.3) | copy-done | bytes 4194328
  155.7 32.7 %shard_map.74 = bf16[4,512,1024]{2,1,0:T(8,128)(2,1)} custom-call(s32[4]{0:T(128)S(1)} %get-tuple-element.5.wild_ref, s32[4]{0:T(128)S(1)} %select_reduce_fusion.length_ref, bf16[4,512,1024]{2,1,0:T(8,128)(2,1)S(1)} %copy-done.1, bf16[8,4,64,1024]{3,2,1,0:T(8,128)(2,1)S(1)} %copy-done.3, ...), custom_call_target="tpu_custom_call", output_to_operand_aliasing={{}: (5, {})} | custom-call | flops 4294967296 | bytes 8388608 | tf_op jit(solution)/shard_map/pallas_call | solution.py:69
  (6 shorter events, 0.0 us)
Async XLA Ops:
  6.5 37.6 %all-gather.4.cloned.1.call-start = ((), (), s32[]{:S(2)}) async-start(), calls=%async_computation | async-start | bytes 3145728 | tf_op jit(solution)/shard_map/all_gather | solution.py:102
  7.3 96.5 %all-gather.8.cloned.1.call-start = ((), (), s32[]{:S(2)}) async-start(), calls=%async_computation.2 | async-start | bytes 4718592 | tf_op jit(solution)/shard_map/all_gather | solution.py:114
  56.3 95.1 %all-gather.6.cloned.1.call-start = ((), (), s32[]{:S(2)}) async-start(), calls=%async_computation.1 | async-start | bytes 4718592 | tf_op jit(solution)/shard_map/all_gather | solution.py:114
  59.8 4.5 %copy-start.4 = (s32[4]{0:T(128)S(1)}, s32[4]{0:T(128)}, u32[]{:S(2)}) copy-start(s32[4]{0:T(128)} %param.13) | copy-start | bytes 52
  59.8 4.8 %copy-start.5 = (s32[4]{0:T(128)S(1)}, s32[4]{0:T(128)}, u32[]{:S(2)}) copy-start(s32[4]{0:T(128)} %param.12) | copy-start | bytes 52
  103.7 2.2 %copy-start = (bf16[4,512,1024]{2,1,0:T(8,128)(2,1)S(1)}, bf16[4,512,1024]{2,1,0:T(8,128)(2,1)}, u32[]{:S(2)}) copy-start(bf16[4,512,1024]{2,1,0:T(8,128)(2,1)} %q_ref.3) | copy-start | bytes 12582916
  105.9 2.2 %copy-start.2 = (bf16[8,4,64,1024]{3,2,1,0:T(8,128)(2,1)S(1)}, bf16[8,4,64,1024]{3,2,1,0:T(8,128)(2,1)}, u32[]{:S(2)}) copy-start(bf16[8,4,64,1024]{3,2,1,0:T(8,128)(2,1)} %all-gather.8.cloned.1.call-done.k_ref.v_ref) | copy-start | bytes 12582916
  151.4 2.2 %copy-start.1 = (bf16[4,512,1024]{2,1,0:T(8,128)(2,1)S(1)}, bf16[4,512,1024]{2,1,0:T(8,128)(2,1)}, u32[]{:S(2)}) copy-start(bf16[4,512,1024]{2,1,0:T(8,128)(2,1)} %q_ref.3) | copy-start | bytes 12582916
  153.6 2.2 %copy-start.3 = (bf16[8,4,64,1024]{3,2,1,0:T(8,128)(2,1)S(1)}, bf16[8,4,64,1024]{3,2,1,0:T(8,128)(2,1)}, u32[]{:S(2)}) copy-start(bf16[8,4,64,1024]{3,2,1,0:T(8,128)(2,1)} %all-gather.6.cloned.1.call-done.k_ref.v_ref) | copy-start | bytes 12582916
Sparse Core Ops, SparseCore 0:
  8.9 35.1 all-gather.3
  56.4 47.3 all-gather.7
  105.4 45.9 all-gather.5

commit v2 on v1

--- a/solution.py
+++ b/solution.py
@@ -13,6 +13,11 @@
 PAIR = 2 * HD
 Q_CHUNK = 256
 HEAD_CHUNKS = 2
+ROW_GROUPS = 2
+PIECES = 4
+COUNT_MIN = 4
+COUNT_MAX = 12
+MESH = pl.DeviceIdType.MESH
 
 
 def wild_of_slots(variant_counts, slot_total):
@@ -48,23 +53,12 @@
         o_ref[0, pl.ds(start, Q_CHUNK), :] = jnp.where(row < length, out, 0.0).astype(o_ref.dtype)
 
 
-def attend(own_wild, own_lengths, queries, gathered, previous, chunk):
+def attend(own_wild, own_lengths, queries, gathered):
     slots, _, inner = queries.shape
-    peers, _, part, double = gathered.shape
-    pairs = double // 2 // PAIR
-    base = chunk * pairs
-    kv_block = (peers, 1, part, PAIR)
-    in_specs = [
-        pl.BlockSpec((1, LEN, PAIR), lambda h, s, w, n: (s, 0, base + h)),
-        pl.BlockSpec(kv_block, lambda h, s, w, n: (0, w[s], 0, h)),
-        pl.BlockSpec(kv_block, lambda h, s, w, n: (0, w[s], 0, pairs + h)),
-    ]
-    operands = [own_wild, own_lengths, queries, gathered, gathered]
-    aliases = {}
-    if previous is not None:
-        in_specs.append(pl.BlockSpec(memory_space=pl.ANY))
-        operands.append(previous)
-        aliases = {5: 0}
+    chunks, peers, _, part, double = gathered.shape
+    per_chunk = double // 2 // PAIR
+    pairs = chunks * per_chunk
+    kv_block = (1, peers, 1, part, PAIR)
     elements = slots * pairs * 2 * LEN * LEN
     return pl.pallas_call(
         attend_kernel,
@@ -72,21 +66,265 @@
         grid_spec=pltpu.PrefetchScalarGridSpec(
             num_scalar_prefetch=2,
             grid=(pairs, slots),
-            in_specs=in_specs,
-            out_specs=pl.BlockSpec((1, LEN, PAIR), lambda h, s, w, n: (s, 0, base + h)),
+            in_specs=[
+                pl.BlockSpec((1, LEN, PAIR), lambda h, s, w, n: (s, 0, h)),
+                pl.BlockSpec(kv_block, lambda h, s, w, n: (h // per_chunk, 0, w[s], 0, h % per_chunk)),
+                pl.BlockSpec(kv_block, lambda h, s, w, n: (h // per_chunk, 0, w[s], 0, per_chunk + h % per_chunk)),
+            ],
+            out_specs=pl.BlockSpec((1, LEN, PAIR), lambda h, s, w, n: (s, 0, h)),
         ),
-        input_output_aliases=aliases,
         compiler_params=pltpu.CompilerParams(vmem_limit_bytes=32 << 20),
         cost_estimate=pl.CostEstimate(
             flops=elements * 2 * PAIR * 2, transcendentals=elements, bytes_accessed=slots * pairs * LEN * PAIR * 8
         ),
-    )(*operands)
+    )(own_wild, own_lengths, queries, gathered, gathered)
+
+
+def exchange_kernel(
+    sizes, x_ref, gain_ref, kw_ref, vw_ref, out_ref, x_full, weights, gained, scale, own,
+    x_sems, w_sems, x_send, x_recv, z_send, z_recv, r_send, r_recv, o_sems,
+):
+    seq_size, mp_size, rep_size, slot_local, wild_total, part = sizes
+    z, m, r = lax.axis_index("seq"), lax.axis_index("mp"), lax.axis_index("rep")
+    row_total, part_width = x_ref.shape
+    width = kw_ref.shape[1] // HEAD_CHUNKS
+    group_rows = row_total // ROW_GROUPS
+    piece_wilds = wild_total // PIECES
+    group_pieces = PIECES // ROW_GROUPS
+    group_wilds = wild_total // ROW_GROUPS
+    chip_slots = slot_local * rep_size
+    total_slots = chip_slots * seq_size
+
+    barrier = pltpu.get_barrier_semaphore()
+    for off in range(1, mp_size):
+        pl.semaphore_signal(barrier, 1, device_id={"mp": lax.rem(m + off, mp_size)}, device_id_type=MESH)
+    for off in range(1, rep_size):
+        pl.semaphore_signal(barrier, 1, device_id={"rep": lax.rem(r + off, rep_size)}, device_id_type=MESH)
+
+    @pl.when(z < seq_size - 1)
+    def _():
+        pl.semaphore_signal(barrier, 1, device_id={"seq": z + 1}, device_id_type=MESH)
+
+    @pl.when(z > 0)
+    def _():
+        pl.semaphore_signal(barrier, 1, device_id={"seq": z - 1}, device_id_type=MESH)
+
+    def rows_of(group):
+        return pl.ds(group * group_rows, group_rows)
+
+    def own_copy(group):
+        return pltpu.make_async_copy(
+            x_ref.at[rows_of(group)], x_full.at[m, rows_of(group)], x_sems.at[group]
+        )
+
+    def weight_copy(chunk, which):
+        ref = (kw_ref, vw_ref)[which]
+        return pltpu.make_async_copy(
+            ref.at[:, pl.ds(chunk * width, width)], weights.at[chunk, which], w_sems.at[chunk, which]
+        )
+
+    def feature_copy(group, off, sender):
+        return pltpu.make_async_remote_copy(
+            src_ref=x_ref.at[rows_of(group)],
+            dst_ref=x_full.at[sender, rows_of(group)],
+            send_sem=x_send.at[group, off - 1],
+            recv_sem=x_recv.at[group, off - 1],
+            device_id={"mp": lax.rem(m + off, mp_size)},
+            device_id_type=MESH,
+        )
+
+    for group in range(ROW_GROUPS):
+        own_copy(group).start()
+    for chunk in range(HEAD_CHUNKS):
+        for which in range(2):
+            weight_copy(chunk, which).start()
+    neighbours = (mp_size - 1) + (rep_size - 1) + jnp.where(z > 0, 1, 0) + jnp.where(z < seq_size - 1, 1, 0)
+    pl.semaphore_wait(barrier, neighbours)
+    for group in range(ROW_GROUPS):
+        for off in range(1, mp_size):
+            feature_copy(group, off, m).start()
+
+    def lowest(piece):
+        wild = piece * piece_wilds
+        return max(COUNT_MIN * wild, total_slots - COUNT_MAX * (wild_total - wild))
+
+    def highest(piece):
+        wild = (piece + 1) * piece_wilds
+        return min(COUNT_MAX * wild, total_slots - COUNT_MIN * (wild_total - wild))
+
+    def wanted_right(chip, piece):
+        return highest(piece) > chip * chip_slots
+
+    def wanted_left(chip, piece):
+        return lowest(piece) < (chip + 1) * chip_slots
+
+    def slab(chunk, origin, core, piece):
+        return out_ref.at[chunk, origin, core, pl.ds(piece * piece_wilds, piece_wilds)]
+
+    def own_slab(chunk, piece):
+        return own.at[chunk, pl.ds(piece * piece_wilds, piece_wilds)]
+
+    def hop(way, step, chunk, piece, origin, from_own):
+        ahead = z + 1 if way == 0 else z - 1
+        return pltpu.make_async_remote_copy(
+            src_ref=own_slab(chunk, piece) if from_own else slab(chunk, origin, r, piece),
+            dst_ref=slab(chunk, origin, r, piece),
+            send_sem=z_send.at[way, step, chunk, piece],
+            recv_sem=z_recv.at[way, step, chunk, piece],
+            device_id={"seq": ahead},
+            device_id_type=MESH,
+        )
+
+    def twin(off, way, step, chunk, piece, origin, core, from_own):
+        return pltpu.make_async_remote_copy(
+            src_ref=own_slab(chunk, piece) if from_own else slab(chunk, origin, core, piece),
+            dst_ref=slab(chunk, origin, core, piece),
+            send_sem=r_send.at[off - 1, way, step, chunk, piece],
+            recv_sem=r_recv.at[off - 1, way, step, chunk, piece],
+            device_id={"rep": lax.rem(r + off, rep_size)},
+            device_id_type=MESH,
+        )
+
+    def origin_of(way, step):
+        return z - step if way == 0 else z + step
+
+    def sends(way, step, piece):
+        if way == 0:
+            return (z - step >= 0) & (z < seq_size - 1) & wanted_right(z + 1, piece)
+        return (z + step < seq_size) & (z > 0) & wanted_left(z - 1, piece)
+
+    def arrives(way, step, piece):
+        if way == 0:
+            return (z - step >= 0) & wanted_right(z, piece)
+        return (z + step < seq_size) & wanted_left(z, piece)
+
+    def twin_moves(way, step, piece):
+        near = wanted_right(z, piece) & wanted_left(z, piece)
+        return near if step == 0 else near & arrives(way, step, piece)
+
+    def first_sends(group, chunk):
+        for piece in range(group * group_pieces, (group + 1) * group_pieces):
+            for way in range(2):
+                pl.when(sends(way, 0, piece))(hop(way, 0, chunk, piece, z, True).start)
+            for off in range(1, rep_size):
+                pl.when(twin_moves(0, 0, piece))(twin(off, 0, 0, chunk, piece, z, r, True).start)
+            pltpu.make_async_copy(
+                own_slab(chunk, piece), slab(chunk, z, r, piece), o_sems.at[chunk, piece]
+            ).start()
+
+    def forward(group, chunk, step):
+        for piece in range(group * group_pieces, (group + 1) * group_pieces):
+            for way in range(2):
+                origin = origin_of(way, step)
+
+                @pl.when(arrives(way, step, piece))
+                def _():
+                    hop(way, step - 1, chunk, piece, origin, False).wait_recv()
+
+                if step < seq_size - 1:
+                    pl.when(sends(way, step, piece))(hop(way, step, chunk, piece, origin, False).start)
+                for off in range(1, rep_size):
+                    pl.when(twin_moves(way, step, piece))(
+                        twin(off, way, step, chunk, piece, origin, r, False).start
+                    )
+
+    def project(group, chunk):
+        rows = rows_of(group)
+        if chunk == 0:
+            own_copy(group).wait()
+            for off in range(1, mp_size):
+                feature_copy(group, off, lax.rem(m - off + mp_size, mp_size)).wait_recv()
+            squares = jnp.zeros((group_rows, 1), jnp.float32)
+            for block in range(mp_size):
+                columns = pl.ds(block * part_width, part_width)
+                wide = x_full[block, rows, :].astype(jnp.float32)
+                squares = squares + jnp.sum(wide * wide, axis=1, keepdims=True)
+                gained[:, columns] = (wide * gain_ref[:, columns]).astype(jnp.bfloat16)
+            scale[...] = lax.rsqrt(squares / D + 1e-06)
+        for which in range(2):
+            if group == 0:
+                weight_copy(chunk, which).wait()
+            total = jnp.dot(gained[...], weights[chunk, which], preferred_element_type=jnp.float32)
+            own[chunk, pl.ds(group * group_wilds, group_wilds), :, pl.ds(which * width, width)] = (
+                (scale[...] * total).astype(jnp.bfloat16).reshape(group_wilds, part, width)
+            )
+
+    tasks = [(group, chunk) for group in range(ROW_GROUPS) for chunk in range(HEAD_CHUNKS)]
+    for time in range(len(tasks) + 2 * (seq_size - 1)):
+        if time < len(tasks):
+            project(*tasks[time])
+            first_sends(*tasks[time])
+        for step in range(seq_size - 1, 0, -1):
+            if 0 <= time - 2 * step < len(tasks):
+                forward(*tasks[time - 2 * step], step)
+
+    for group in range(ROW_GROUPS):
+        for off in range(1, mp_size):
+            feature_copy(group, off, m).wait_send()
+    for chunk in range(HEAD_CHUNKS):
+        for piece in range(PIECES):
+            pltpu.make_async_copy(
+                own_slab(chunk, piece), slab(chunk, z, r, piece), o_sems.at[chunk, piece]
+            ).wait()
+            for step in range(seq_size):
+                for way in range(2):
+                    origin = origin_of(way, step)
+                    if step < seq_size - 1:
+                        pl.when(sends(way, step, piece))(
+                            hop(way, step, chunk, piece, origin, step == 0).wait_send
+                        )
+                    if step == 0 and way == 1:
+                        continue
+                    for off in range(1, rep_size):
+                        other = lax.rem(r - off + rep_size, rep_size)
+
+                        @pl.when(twin_moves(way, step, piece))
+                        def _():
+                            twin(off, way, step, chunk, piece, origin, r, step == 0).wait_send()
+                            twin(off, way, step, chunk, piece, origin, other, False).wait_recv()
+
+
+def exchange(encoder_rows, norm_gain, key_weight, value_weight, slot_local):
+    wild_total, part, part_width = encoder_rows.shape
+    row_total = wild_total * part
+    depth, inner = key_weight.shape
+    seq_size, mp_size, rep_size = (lax.axis_size(name) for name in ("seq", "mp", "rep"))
+    width = inner // HEAD_CHUNKS
+    dma = pltpu.SemaphoreType.DMA
+    peers_mp, peers_rep = max(mp_size - 1, 1), max(rep_size - 1, 1)
+    whole = pl.BlockSpec(memory_space=pltpu.VMEM)
+    place = pl.BlockSpec(memory_space=pl.ANY)
+    return pl.pallas_call(
+        functools.partial(exchange_kernel, (seq_size, mp_size, rep_size, slot_local, wild_total, part)),
+        out_shape=jax.ShapeDtypeStruct(
+            (HEAD_CHUNKS, seq_size, rep_size, wild_total, part, 2 * width), jnp.bfloat16
+        ),
+        in_specs=[place, whole, place, place],
+        out_specs=place,
+        scratch_shapes=[
+            pltpu.VMEM((mp_size, row_total, part_width), jnp.bfloat16),
+            pltpu.VMEM((HEAD_CHUNKS, 2, depth, width), jnp.bfloat16),
+            pltpu.VMEM((row_total // ROW_GROUPS, depth), jnp.bfloat16),
+            pltpu.VMEM((row_total // ROW_GROUPS, 1), jnp.float32),
+            pltpu.VMEM((HEAD_CHUNKS, wild_total, part, 2 * width), jnp.bfloat16),
+            dma((ROW_GROUPS,)),
+            dma((HEAD_CHUNKS, 2)),
+            dma((ROW_GROUPS, peers_mp)),
+            dma((ROW_GROUPS, peers_mp)),
+            dma((2, seq_size, HEAD_CHUNKS, PIECES)),
+            dma((2, seq_size, HEAD_CHUNKS, PIECES)),
+            dma((peers_rep, 2, seq_size, HEAD_CHUNKS, PIECES)),
+            dma((peers_rep, 2, seq_size, HEAD_CHUNKS, PIECES)),
+            dma((HEAD_CHUNKS, PIECES)),
+        ],
+        compiler_params=pltpu.CompilerParams(
+            collective_id=0, has_side_effects=True, vmem_limit_bytes=40 << 20
+        ),
+    )(encoder_rows.reshape(row_total, part_width), norm_gain.astype(jnp.float32)[None, :], key_weight, value_weight)
 
 
 def local(encoder_rows, norm_gain, key_weight, value_weight, queries, wild_lengths, variant_counts):
-    wild_total, part_length, part_width = encoder_rows.shape
-    row_total = wild_total * part_length
-    inner_local = key_weight.shape[1]
+    wild_total = encoder_rows.shape[0]
     seq_size = lax.axis_size("seq")
     rep_size = lax.axis_size("rep")
     peer_total = seq_size * rep_size
@@ -99,23 +337,9 @@
         jnp.where(own_wild[:, None] == wild_number[None, :], wild_lengths[None, :], 0), axis=1
     )
     own_wild = jnp.minimum(own_wild, wild_total - 1)
-    rows = lax.all_gather(encoder_rows, "mp", axis=2, tiled=True).reshape(row_total, -1).astype(jnp.float32)
-    gained = (rows * norm_gain.astype(jnp.float32)[None, :]).astype(jnp.bfloat16)
-    inverse_rms = lax.rsqrt(jnp.sum(rows * rows, axis=1) / D + 1e-06)[:, None]
-    width = inner_local // HEAD_CHUNKS
-    shared = []
-    for chunk in range(HEAD_CHUNKS):
-        columns = slice(chunk * width, (chunk + 1) * width)
-        parts = []
-        for weight in (key_weight, value_weight):
-            total = jnp.dot(gained, weight[:, columns], preferred_element_type=jnp.float32)
-            parts.append((inverse_rms * total).astype(jnp.bfloat16))
-        paired = jnp.concatenate(parts, axis=1).reshape(wild_total, part_length, 2 * width)
-        shared.append(lax.all_gather(paired, ("seq", "rep"), axis=0))
-    context = None
-    for chunk in range(HEAD_CHUNKS):
-        context = attend(own_wild, own_lengths, queries, shared[chunk], context, chunk)
-    return context
+    shared = exchange(encoder_rows, norm_gain, key_weight, value_weight, slot_local)
+    gathered = shared.reshape((HEAD_CHUNKS, peer_total) + shared.shape[3:])
+    return attend(own_wild, own_lengths, queries, gathered)
 
 
 def solution(mesh):

time: 195 us -> 133 us (0.68)
  the two profiles are of different devices: /device:TPU:1 before, /device:TPU:29 now
where the time goes in v2:
time: 133 us
  Pallas kernels  129 us (97%)
  other arithmetic  2.53 us (2%)
    pallas_call x1, Pallas kernels, exchange(): pl.pallas_call(functools.partial(exchange_kernel, (seq_size, mp_size, rep...  65.2 us
    pallas_call x1, Pallas kernels, attend(): pl.pallas_call(attend_kernel, out_shape=jax.ShapeDtypeStruct(queries.shap...  64 us

profile of v2, /device:TPU:29, one launch (start us, length us, event | category | flops | bytes accessed | tf_op | source)
XLA Modules:
  0.0 133.0 jit_solution(2138812968768955379)
XLA Ops:
  0.0 0.8 reduce-window.8
  0.8 0.1 convert_reduce_fusion
  0.9 0.1 broadcast_minimum_fusion
  1.0 0.8 select_reduce_fusion.length_ref
  1.8 0.7 broadcast_in_dim.26
  2.5 0.0 copy-start
  2.5 1.2 copy-done
  3.8 0.0 copy-start.1
  3.8 65.2 %shard_map.73 = bf16[2,4,2,4,64,1024]{5,4,3,2,1,0:T(8,128)(2,1)S(1)} custom-call(bf16[256,2048]{1,0:T(8,128)(2,1)S(1)} %bitcast.7, f32[1,4096]{1,0:T(1,128)S(1)} %bitcast.8, bf16[4096,1024]{1,0:T(8,128)(2,1)} %kw_ref.1, bf16[4096,1024]{1,0:T(8,128)(2,1)} %vw_ref.1), custom_call_target="tpu_custom_call" | custom-call | tf_op jit(solution)/shard_map/pallas_call | solution.py:297
  69.0 0.0 copy-done.1
  69.0 64.0 %shard_map.74 = bf16[4,512,1024]{2,1,0:T(8,128)(2,1)} custom-call(s32[4]{0:T(128)S(1)} %get-tuple-element.5.wild_ref, s32[4]{0:T(128)S(1)} %select_reduce_fusion.length_ref, bf16[4,512,1024]{2,1,0:T(8,128)(2,1)S(1)} %copy-done.1, bf16[2,8,4,64,1024]{4,3,2,1,0:T(8,128)(2,1)S(1)} %bitcast.5, bf16[2,8,4,64,1024]{4,3,2,1,0:T(8,128)(2,1)S(1)} %bitcast.6), custom_call_target="tpu_custom_call" | custom-call | flops 8589934592 | bytes 16777216 | tf_op jit(solution)/shard_map/pallas_call | solution.py:63
Async XLA Ops:
  2.5 1.2 copy-start
  3.8 65.2 %copy-start.1 = (bf16[4,512,1024]{2,1,0:T(8,128)(2,1)S(1)}, bf16[4,512,1024]{2,1,0:T(8,128)(2,1)}, u32[]{:S(2)}) copy-start(bf16[4,512,1024]{2,1,0:T(8,128)(2,1)} %q_ref.1) | copy-start | bytes 12582916

commit v3 on v2

--- a/solution.py
+++ b/solution.py
@@ -11,7 +11,7 @@
 HD = 64
 LEN = 512
 PAIR = 2 * HD
-Q_CHUNK = 256
+STEP_PAIRS = 4
 HEAD_CHUNKS = 2
 ROW_GROUPS = 2
 PIECES = 4
@@ -26,56 +26,77 @@
     return jnp.sum((running_end[None, :] <= slot_number[:, None]).astype(jnp.int32), axis=1)
 
 
-def attend_kernel(wild_ref, length_ref, q_ref, k_ref, v_ref, *rest):
-    o_ref = rest[-1]
+def attend_kernel(wild_ref, length_ref, q_ref, k_ref, v_ref, o_ref):
     length = length_ref[pl.program_id(1)]
-    keys = k_ref[...].reshape(LEN, PAIR)
-    values = v_ref[...].reshape(LEN, PAIR)
-    lane = lax.broadcasted_iota(jnp.int32, (Q_CHUNK, PAIR), 1)
-    valid = lax.broadcasted_iota(jnp.int32, (Q_CHUNK, LEN), 1) < length
-    for start in range(0, LEN, Q_CHUNK):
-        query = q_ref[0, pl.ds(start, Q_CHUNK), :]
+    items = [(pair, head) for pair in range(q_ref.shape[2] // PAIR) for head in range(2)]
+    lane = lax.broadcasted_iota(jnp.int32, (LEN, PAIR), 1)
+
+    def columns_of(pair):
+        return pl.ds(pair * PAIR, PAIR)
+
+    def score(pair, head):
+        keys = k_ref[0, :, 0, :, columns_of(pair)].reshape(LEN, PAIR)
+        query = q_ref[0, :, columns_of(pair)]
+        own_lanes = lane < HD if head == 0 else lane >= HD
+        return lax.dot_general(
+            jnp.where(own_lanes, query, jnp.zeros_like(query)),
+            keys,
+            (((1,), (1,)), ((), ())),
+            preferred_element_type=jnp.float32,
+        )
+
+    def attend_pairs(masked):
+        following = score(*items[0])
         outs = []
-        for head in range(2):
-            own_lanes = lane < HD if head == 0 else lane >= HD
-            masked_query = jnp.where(own_lanes, query, jnp.zeros_like(query))
-            scores = lax.dot_general(
-                masked_query, keys, (((1,), (1,)), ((), ())), preferred_element_type=jnp.float32
-            )
-            scores = jnp.where(valid, scores, jnp.float32(-1e30))
+        for at, (pair, head) in enumerate(items):
+            scores = following
+            if at + 1 < len(items):
+                following = score(*items[at + 1])
+            if masked:
+                valid = lax.broadcasted_iota(jnp.int32, (LEN, LEN), 1) < length
+                scores = jnp.where(valid, scores, jnp.float32(-1e30))
             maximum = jnp.max(scores, axis=1, keepdims=True)
             weights = jnp.exp(scores - maximum)
             inverse = 1.0 / jnp.sum(weights, axis=1, keepdims=True)
             probs = (weights * inverse).astype(jnp.bfloat16)
+            values = v_ref[0, :, 0, :, columns_of(pair)].reshape(LEN, PAIR)
             outs.append(jnp.dot(probs, values, preferred_element_type=jnp.float32))
-        out = jnp.where(lane < HD, outs[0], outs[1])
-        row = start + lax.broadcasted_iota(jnp.int32, (Q_CHUNK, PAIR), 0)
-        o_ref[0, pl.ds(start, Q_CHUNK), :] = jnp.where(row < length, out, 0.0).astype(o_ref.dtype)
+            if head == 1:
+                out = jnp.where(lane < HD, outs[0], outs[1])
+                outs = []
+                if masked:
+                    row = lax.broadcasted_iota(jnp.int32, (LEN, PAIR), 0)
+                    out = jnp.where(row < length, out, 0.0)
+                o_ref[0, :, columns_of(pair)] = out.astype(o_ref.dtype)
+
+    pl.when(length < LEN)(lambda: attend_pairs(True))
+    pl.when(length >= LEN)(lambda: attend_pairs(False))
 
 
 def attend(own_wild, own_lengths, queries, gathered):
     slots, _, inner = queries.shape
     chunks, peers, _, part, double = gathered.shape
-    per_chunk = double // 2 // PAIR
-    pairs = chunks * per_chunk
-    kv_block = (1, peers, 1, part, PAIR)
-    elements = slots * pairs * 2 * LEN * LEN
+    block = min(STEP_PAIRS * PAIR, double // 2)
+    per_chunk = double // 2 // block
+    steps = chunks * per_chunk
+    kv_block = (1, peers, 1, part, block)
+    elements = slots * (inner // HD) * LEN * LEN
     return pl.pallas_call(
         attend_kernel,
         out_shape=jax.ShapeDtypeStruct(queries.shape, jnp.bfloat16),
         grid_spec=pltpu.PrefetchScalarGridSpec(
             num_scalar_prefetch=2,
-            grid=(pairs, slots),
+            grid=(steps, slots),
             in_specs=[
-                pl.BlockSpec((1, LEN, PAIR), lambda h, s, w, n: (s, 0, h)),
+                pl.BlockSpec((1, LEN, block), lambda h, s, w, n: (s, 0, h)),
                 pl.BlockSpec(kv_block, lambda h, s, w, n: (h // per_chunk, 0, w[s], 0, h % per_chunk)),
                 pl.BlockSpec(kv_block, lambda h, s, w, n: (h // per_chunk, 0, w[s], 0, per_chunk + h % per_chunk)),
             ],
-            out_specs=pl.BlockSpec((1, LEN, PAIR), lambda h, s, w, n: (s, 0, h)),
+            out_specs=pl.BlockSpec((1, LEN, block), lambda h, s, w, n: (s, 0, h)),
         ),
-        compiler_params=pltpu.CompilerParams(vmem_limit_bytes=32 << 20),
+        compiler_params=pltpu.CompilerParams(vmem_limit_bytes=48 << 20),
         cost_estimate=pl.CostEstimate(
-            flops=elements * 2 * PAIR * 2, transcendentals=elements, bytes_accessed=slots * pairs * LEN * PAIR * 8
+            flops=elements * 2 * PAIR * 2, transcendentals=elements, bytes_accessed=slots * LEN * inner * 8
         ),
     )(own_wild, own_lengths, queries, gathered, gathered)
 

time: 133 us -> 103 us (0.77)
  Pallas kernels: 129 us -> 96.1 us
  local copies, waits for them, and re-layouts: 1.23 us -> 4.44 us
    pallas_call x1, Pallas kernels: 64 us -> 30.9 us  [attend(): pl.pallas_call(attend_kernel, out_shape=jax.ShapeDtypeStruct(queries.shap...]
    unnamed x4 -> x6, local copies, waits for them, and re-layouts: 1.23 us -> 4.44 us
where the time goes in v3:
time: 103 us
  Pallas kernels  96.1 us (93%)
  local copies, waits for them, and re-layouts  4.44 us (4%)
  other arithmetic  2.53 us (2%)
    pallas_call x1, Pallas kernels, exchange(): pl.pallas_call(functools.partial(exchange_kernel, (seq_size, mp_size, rep...  65.2 us
    pallas_call x1, Pallas kernels, attend(): pl.pallas_call(attend_kernel, out_shape=jax.ShapeDtypeStruct(queries.shap...  30.9 us
    unnamed x6, local copies, waits for them, and re-layouts  4.44 us

profile of v3, /device:TPU:29, one launch (start us, length us, event | category | flops | bytes accessed | tf_op | source)
XLA Modules:
  0.0 103.1 jit_solution(15305169226813665404)
XLA Ops:
  0.0 0.8 reduce-window.8
  0.8 0.1 convert_reduce_fusion
  0.9 0.1 broadcast_minimum_fusion
  1.0 0.8 select_reduce_fusion.length_ref
  1.8 0.7 broadcast_in_dim.26
  2.5 0.0 copy-start.1
  2.5 1.2 %copy-done.1 = bf16[4,64,2048]{2,1,0:T(8,128)(2,1)S(1)} copy-done((bf16[4,64,2048]{2,1,0:T(8,128)(2,1)S(1)}, bf16[4,64,2048]{2,1,0:T(8,128)(2,1)}, u32[]{:S(2)}) %copy-start.1) | copy-done | bytes 1048600
  3.8 0.0 copy-start.2
  3.8 65.2 %shard_map.73 = bf16[2,4,2,4,64,1024]{5,4,3,2,1,0:T(8,128)(2,1)S(1)} custom-call(bf16[256,2048]{1,0:T(8,128)(2,1)S(1)} %bitcast.7, f32[1,4096]{1,0:T(1,128)S(1)} %bitcast.8, bf16[4096,1024]{1,0:T(8,128)(2,1)} %kw_ref.1, bf16[4096,1024]{1,0:T(8,128)(2,1)} %vw_ref.1), custom_call_target="tpu_custom_call" | custom-call | tf_op jit(solution)/shard_map/pallas_call | solution.py:318
  69.0 0.0 copy-start
  69.0 3.2 %copy-done = bf16[2,4,2,4,64,1024]{5,4,3,2,1,0:T(8,128)(2,1)} copy-done((bf16[2,4,2,4,64,1024]{5,4,3,2,1,0:T(8,128)(2,1)}, bf16[2,4,2,4,64,1024]{5,4,3,2,1,0:T(8,128)(2,1)S(1)}, u32[]{:S(2)}) %copy-start) | copy-done | bytes 8388632
  72.2 0.0 copy-done.2
  72.2 30.9 %shard_map.74 = bf16[4,512,1024]{2,1,0:T(8,128)(2,1)} custom-call(s32[4]{0:T(128)S(1)} %get-tuple-element.5.wild_ref, s32[4]{0:T(128)S(1)} %select_reduce_fusion.length_ref, bf16[4,512,1024]{2,1,0:T(8,128)(2,1)S(1)} %copy-done.2, bf16[2,8,4,64,1024]{4,3,2,1,0:T(8,128)(2,1)} %bitcast.5, bf16[2,8,4,64,1024]{4,3,2,1,0:T(8,128)(2,1)} %bitcast.6), custom_call_target="tpu_custom_call" | custom-call | flops 8589934592 | bytes 16777216 | tf_op jit(solution)/shard_map/pallas_call | solution.py:84
Async XLA Ops:
  2.5 1.2 %copy-start.1 = (bf16[4,64,2048]{2,1,0:T(8,128)(2,1)S(1)}, bf16[4,64,2048]{2,1,0:T(8,128)(2,1)}, u32[]{:S(2)}) copy-start(bf16[4,64,2048]{2,1,0:T(8,128)(2,1)} %param.7) | copy-start | bytes 3145732
  3.8 68.5 %copy-start.2 = (bf16[4,512,1024]{2,1,0:T(8,128)(2,1)S(1)}, bf16[4,512,1024]{2,1,0:T(8,128)(2,1)}, u32[]{:S(2)}) copy-start(bf16[4,512,1024]{2,1,0:T(8,128)(2,1)} %q_ref.1) | copy-start | bytes 12582916
  69.0 3.2 %copy-start = (bf16[2,4,2,4,64,1024]{5,4,3,2,1,0:T(8,128)(2,1)}, bf16[2,4,2,4,64,1024]{5,4,3,2,1,0:T(8,128)(2,1)S(1)}, u32[]{:S(2)}) copy-start(bf16[2,4,2,4,64,1024]{5,4,3,2,1,0:T(8,128)(2,1)S(1)} %shard_map.73) | copy-start | bytes 25165828

commit v4 on v3

--- a/solution.py
+++ b/solution.py
@@ -13,7 +13,7 @@
 PAIR = 2 * HD
 STEP_PAIRS = 4
 HEAD_CHUNKS = 2
-ROW_GROUPS = 2
+ROW_GROUPS = 4
 PIECES = 4
 COUNT_MIN = 4
 COUNT_MAX = 12
@@ -94,7 +94,7 @@
             ],
             out_specs=pl.BlockSpec((1, LEN, block), lambda h, s, w, n: (s, 0, h)),
         ),
-        compiler_params=pltpu.CompilerParams(vmem_limit_bytes=48 << 20),
+        compiler_params=pltpu.CompilerParams(vmem_limit_bytes=60 << 20),
         cost_estimate=pl.CostEstimate(
             flops=elements * 2 * PAIR * 2, transcendentals=elements, bytes_accessed=slots * LEN * inner * 8
         ),

time: 103 us -> 101 us (0.981)
  Pallas kernels: 96.1 us -> 92.4 us
    pallas_call x1, Pallas kernels: 65.2 us -> 61.5 us  [exchange(): pl.pallas_call(functools.partial(exchange_kernel, (seq_size, mp_size, rep...]
    unnamed x6 -> x4, local copies, waits for them, and re-layouts: 4.44 us -> 4.44 us
where the time goes in v4:
time: 101 us; the launch traced here: 100 us
  Pallas kernels  92.4 us (91%)
  local copies, waits for them, and re-layouts  4.44 us (4%)
  other arithmetic  3.53 us (3%)
    pallas_call x1, Pallas kernels, exchange(): pl.pallas_call(functools.partial(exchange_kernel, (seq_size, mp_size, rep...  61.5 us
    pallas_call x1, Pallas kernels, attend(): pl.pallas_call(attend_kernel, out_shape=jax.ShapeDtypeStruct(queries.shap...  31 us
    unnamed x4, local copies, waits for them, and re-layouts  4.44 us

profile of v4, /device:TPU:29, one launch (start us, length us, event | category | flops | bytes accessed | tf_op | source)
XLA Modules:
  0.0 100.4 jit_solution(8956402070885330983)
XLA Ops:
  0.0 0.8 reduce-window.8
  0.8 0.1 convert_reduce_fusion
  0.9 0.6 broadcast_minimum_fusion
  1.5 1.4 %select_reduce_fusion.length_ref = s32[4]{0:T(128)} fusion(s32[4]{0:T(128)} %param.12, s32[4]{0:T(128)S(1)} %get-tuple-element.6), kind=kLoop, calls=%fused_computation | loop fusion | flops 44 | bytes 48 | tf_op jit(solution)/shard_map/reduce_sum | solution.py:357
  2.8 0.7 broadcast_in_dim.26
  3.5 0.0 copy-start.1
  3.5 1.2 %copy-done.1 = bf16[4,64,2048]{2,1,0:T(8,128)(2,1)S(1)} copy-done((bf16[4,64,2048]{2,1,0:T(8,128)(2,1)S(1)}, bf16[4,64,2048]{2,1,0:T(8,128)(2,1)}, u32[]{:S(2)}) %copy-start.1) | copy-done | bytes 1048600
  4.8 61.5 %shard_map.73 = bf16[2,4,2,4,64,1024]{5,4,3,2,1,0:T(8,128)(2,1)S(1)} custom-call(bf16[256,2048]{1,0:T(8,128)(2,1)S(1)} %bitcast.7, f32[1,4096]{1,0:T(1,128)S(1)} %bitcast.8, bf16[4096,1024]{1,0:T(8,128)(2,1)} %kw_ref.1, bf16[4096,1024]{1,0:T(8,128)(2,1)} %vw_ref.1), custom_call_target="tpu_custom_call" | custom-call | tf_op jit(solution)/shard_map/pallas_call | solution.py:318
  66.2 0.0 copy-start
  66.2 3.2 %copy-done = bf16[2,4,2,4,64,1024]{5,4,3,2,1,0:T(8,128)(2,1)} copy-done((bf16[2,4,2,4,64,1024]{5,4,3,2,1,0:T(8,128)(2,1)}, bf16[2,4,2,4,64,1024]{5,4,3,2,1,0:T(8,128)(2,1)S(1)}, u32[]{:S(2)}) %copy-start) | copy-done | bytes 8388632
  69.4 31.0 %shard_map.74 = bf16[4,512,1024]{2,1,0:T(8,128)(2,1)} custom-call(s32[4]{0:T(128)} %get-tuple-element.5.wild_ref, s32[4]{0:T(128)} %select_reduce_fusion.length_ref, bf16[4,512,1024]{2,1,0:T(8,128)(2,1)} %q_ref.1, bf16[2,8,4,64,1024]{4,3,2,1,0:T(8,128)(2,1)} %bitcast.5, bf16[2,8,4,64,1024]{4,3,2,1,0:T(8,128)(2,1)} %bitcast.6), custom_call_target="tpu_custom_call" | custom-call | flops 8589934592 | bytes 16777216 | tf_op jit(solution)/shard_map/pallas_call | solution.py:84
Async XLA Ops:
  3.5 1.2 %copy-start.1 = (bf16[4,64,2048]{2,1,0:T(8,128)(2,1)S(1)}, bf16[4,64,2048]{2,1,0:T(8,128)(2,1)}, u32[]{:S(2)}) copy-start(bf16[4,64,2048]{2,1,0:T(8,128)(2,1)} %param.7) | copy-start | bytes 3145732
  66.2 3.2 %copy-start = (bf16[2,4,2,4,64,1024]{5,4,3,2,1,0:T(8,128)(2,1)}, bf16[2,4,2,4,64,1024]{5,4,3,2,1,0:T(8,128)(2,1)S(1)}, u32[]{:S(2)}) copy-start(bf16[2,4,2,4,64,1024]{5,4,3,2,1,0:T(8,128)(2,1)S(1)} %shard_map.73) | copy-start | bytes 25165828

commit v5 on v4

--- a/solution.py
+++ b/solution.py
@@ -94,7 +94,7 @@
             ],
             out_specs=pl.BlockSpec((1, LEN, block), lambda h, s, w, n: (s, 0, h)),
         ),
-        compiler_params=pltpu.CompilerParams(vmem_limit_bytes=60 << 20),
+        compiler_params=pltpu.CompilerParams(vmem_limit_bytes=32 << 20),
         cost_estimate=pl.CostEstimate(
             flops=elements * 2 * PAIR * 2, transcendentals=elements, bytes_accessed=slots * LEN * inner * 8
         ),

time: 101 us -> 95.2 us (0.943)
  local copies, waits for them, and re-layouts: 4.44 us -> 1.23 us
  Pallas kernels: 92.4 us -> 91.2 us
    unnamed x4, local copies, waits for them, and re-layouts: 4.44 us -> 1.23 us
    pallas_call x1, Pallas kernels: 31 us -> 29.7 us  [attend(): pl.pallas_call(attend_kernel, out_shape=jax.ShapeDtypeStruct(queries.shap...]
where the time goes in v5:
time: 95.2 us; the launch traced here: 95 us
  Pallas kernels  91.2 us (96%)
  other arithmetic  2.53 us (3%)
  local copies, waits for them, and re-layouts  1.23 us (1%)
    pallas_call x1, Pallas kernels, exchange(): pl.pallas_call(functools.partial(exchange_kernel, (seq_size, mp_size, rep...  61.5 us
    pallas_call x1, Pallas kernels, attend(): pl.pallas_call(attend_kernel, out_shape=jax.ShapeDtypeStruct(queries.shap...  29.7 us

profile of v5, /device:TPU:29, one launch (start us, length us, event | category | flops | bytes accessed | tf_op | source)
XLA Modules:
  0.0 95.0 jit_solution(14370374560185869372)
XLA Ops:
  0.0 0.8 reduce-window.8
  0.8 0.1 convert_reduce_fusion
  0.9 0.1 broadcast_minimum_fusion
  1.0 0.8 select_reduce_fusion.length_ref
  1.8 0.7 broadcast_in_dim.26
  2.5 0.0 copy-start
  2.5 1.2 %copy-done = bf16[4,64,2048]{2,1,0:T(8,128)(2,1)S(1)} copy-done((bf16[4,64,2048]{2,1,0:T(8,128)(2,1)S(1)}, bf16[4,64,2048]{2,1,0:T(8,128)(2,1)}, u32[]{:S(2)}) %copy-start) | copy-done | bytes 1048600
  3.8 0.0 copy-start.1
  3.8 61.5 %shard_map.73 = bf16[2,4,2,4,64,1024]{5,4,3,2,1,0:T(8,128)(2,1)S(1)} custom-call(bf16[256,2048]{1,0:T(8,128)(2,1)S(1)} %bitcast.7, f32[1,4096]{1,0:T(1,128)S(1)} %bitcast.8, bf16[4096,1024]{1,0:T(8,128)(2,1)} %kw_ref.1, bf16[4096,1024]{1,0:T(8,128)(2,1)} %vw_ref.1), custom_call_target="tpu_custom_call" | custom-call | tf_op jit(solution)/shard_map/pallas_call | solution.py:318
  65.2 0.0 copy-done.1
  65.2 29.7 %shard_map.74 = bf16[4,512,1024]{2,1,0:T(8,128)(2,1)} custom-call(s32[4]{0:T(128)S(1)} %get-tuple-element.5.wild_ref, s32[4]{0:T(128)S(1)} %select_reduce_fusion.length_ref, bf16[4,512,1024]{2,1,0:T(8,128)(2,1)S(1)} %copy-done.1, bf16[2,8,4,64,1024]{4,3,2,1,0:T(8,128)(2,1)S(1)} %bitcast.5, bf16[2,8,4,64,1024]{4,3,2,1,0:T(8,128)(2,1)S(1)} %bitcast.6), custom_call_target="tpu_custom_call" | custom-call | flops 8589934592 | bytes 16777216 | tf_op jit(solution)/shard_map/pallas_call | solution.py:84
Async XLA Ops:
  2.5 1.2 %copy-start = (bf16[4,64,2048]{2,1,0:T(8,128)(2,1)S(1)}, bf16[4,64,2048]{2,1,0:T(8,128)(2,1)}, u32[]{:S(2)}) copy-start(bf16[4,64,2048]{2,1,0:T(8,128)(2,1)} %param.7) | copy-start | bytes 3145732
  3.8 61.5 %copy-start.1 = (bf16[4,512,1024]{2,1,0:T(8,128)(2,1)S(1)}, bf16[4,512,1024]{2,1,0:T(8,128)(2,1)}, u32[]{:S(2)}) copy-start(bf16[4,512,1024]{2,1,0:T(8,128)(2,1)} %q_ref.1) | copy-start | bytes 12582916
